TPU v7x, 128 devices: a whole 4x4x4 slice. The times are simulated.
128 devices in a mesh: cluster: 16 (over y, x_lo, core), blk: 8 (over x_hi, z).
Axes of the slice: x: 4 (x_hi: 2, x_lo: 2; x = x_hi * 2 + x_lo), y: 4, z: 4, core: 2. Of those that a mesh axis runs over, the one named last changes fastest.
Arguments:
- embeds: bfloat16 [4096, 32, 128], P(('cluster', 'blk')), may hold values from -7 to 7
- labels: int32 [4096, 1], P(('cluster', 'blk')), may hold values from 0 to 15, as said below
- keep: int32 [4096], P(('cluster', 'blk')), may hold values 0 or 1
Outputs:
- dup_score: float32 [4096], P(('cluster', 'blk'))
Inputs may be any that keep to these rules, and one draw needn't show every extreme that they name: `labels`: at most 4 prompts of one device carry the same label, and on every device some label is carried by exactly 4 of its prompts.
All inputs are finite; a program needn't handle non-finite values. No bound on the sum of `keep` on one device may be relied on, other than what follows from the above.
Results may differ from a plain program's by a relative error of at most 0.0003.
Values may be sent and summed in bfloat16 or wider, within the bound.
A program may use at most 64 MiB of HBM per device.

v0:
```python
import jax
import jax.numpy as jnp
from jax import lax
from jax.sharding import PartitionSpec as P

SLOTS = 64
group_size = 8


def pair_scores(residents, visitors):
    length = residents.shape[1]
    width = residents.shape[2]
    visiting = visitors.shape[0]
    flat_visitors = visitors.reshape(visiting * length, width)
    grouped = residents.reshape(residents.shape[0] // group_size, group_size * length, width)

    def one_group(queries):
        score_tile = lax.dot_general(
            queries, flat_visitors, (((1,), (1,)), ((), ())), preferred_element_type=jnp.float32
        )
        score_tile = score_tile.reshape(group_size, length, visiting, length)
        forward = jnp.sum(jnp.max(score_tile, axis=3), axis=1) / length
        return forward

    result = lax.map(one_group, grouped)
    return result.reshape(-1, visiting)


def body(embeds, labels, keep):
    clusters = lax.axis_size("cluster")
    slot_count = SLOTS
    capacity = slot_count // clusters
    label_list = labels[:, 0]
    onehot = (label_list[:, None] == jnp.arange(clusters, dtype=jnp.int32)[None, :]).astype(
        jnp.int32
    )
    slot_rank = jnp.sum((jnp.cumsum(onehot, axis=0) - onehot) * onehot, axis=1)
    slot_index = label_list * capacity + slot_rank
    keep_float = keep.astype(jnp.float32)
    outgoing = (
        jnp.zeros((slot_count, embeds.shape[1], embeds.shape[2]), jnp.bfloat16)
        .at[slot_index]
        .set(embeds)
    )
    outgoing_flags = (
        jnp.zeros((slot_count,), jnp.bfloat16).at[slot_index].set(keep.astype(jnp.bfloat16))
    )
    members, member_flags = (
        lax.all_to_all(outgoing, "cluster", split_axis=0, concat_axis=0, tiled=True),
        lax.all_to_all(outgoing_flags, "cluster", split_axis=0, concat_axis=0, tiled=True),
    )
    flags = member_flags.astype(jnp.float32)
    own_ids = lax.axis_index("blk") * slot_count + jnp.arange(slot_count, dtype=jnp.int32)
    visitors = lax.all_gather(members, "blk", axis=0, tiled=True)
    visitor_flags = lax.all_gather(member_flags, "blk", axis=0, tiled=True)
    other_ids = jnp.arange(visitors.shape[0], dtype=jnp.int32)
    weights = (own_ids[:, None] != other_ids[None, :]).astype(jnp.float32) * visitor_flags.astype(
        jnp.float32
    )[None, :]
    forward = pair_scores(members, visitors)
    sums = jnp.sum(forward * weights, axis=1)
    counts = jnp.sum(weights, axis=1)
    score = jnp.where(flags > 0, sums / jnp.maximum(counts, 1.0), 0.0)
    returned = lax.all_to_all(score, "cluster", split_axis=0, concat_axis=0, tiled=True)
    return returned[slot_index] * keep_float


def solution(mesh):
    return jax.shard_map(
        body,
        mesh=mesh,
        in_specs=(
            P(("cluster", "blk"), None, None),
            P(("cluster", "blk"), None),
            P(("cluster", "blk")),
        ),
        out_specs=P(("cluster", "blk")),
        check_vma=False,
    )
```

profile of v0, /device:TPU:1, one launch (start us, length us, event | category | flops | bytes accessed | tf_op | source)
XLA Modules:
  0.0 191.4 jit_solution(1213588134446596878)
XLA Ops:
  8.9 2.8 %scatter_fusion = bf16[64,32,128]{2,1,0:T(8,128)(2,1)S(1)} fusion(bf16[64,32,128]{2,1,0:T(8,128)(2,1)S(1)} %broadcast_in_dim.11, s32[32]{0:T(128)S(1)} %fusion.7, bf16[32,32,128]{2,1,0:T(8,128)(2,1)} %param.5), kind=kCustom, calls=%fused_computation.2 | custom fusion | bytes 786560 | tf_op jit(solution)/shard_map/scatter | solution.py:43
  11.7 16.6 %all_to_all.27 = bf16[64,32,128]{2,1,0:T(8,128)(2,1)} all-to-all(bf16[64,32,128]{2,1,0:T(8,128)(2,1)S(1)} %scatter_fusion), channel_id=1, replica_groups=mesh['cluster'=16,'blk'=8] {'cluster'}, dimensions={0} | all-to-all | bytes 1048576 | tf_op jit(solution)/shard_map/all_to_all | solution.py:49
  30.5 4.3 %all-to-all-start = ((bf16[16,4,1]{1,2,0:T(2,128)(2,1)}), bf16[16,4,1]{1,2,0:T(2,128)(2,1)S(1)}, u32[]{:S(2)}, u32[]{:S(2)}) async-start(bf16[16,4,1]{1,2,0:T(2,128)(2,1)} %all_to_all.23), calls=%async_computation | async-start | bytes 16384 | tf_op jit(solution)/shard_map/all_to_all | solution.py:50
  34.9 1.3 dynamic-slice
  36.8 3.6 %all-to-all-done = bf16[16,4,1]{1,2,0:T(2,128)(2,1)S(1)} async-done(((bf16[16,4,1]{1,2,0:T(2,128)(2,1)}), bf16[16,4,1]{1,2,0:T(2,128)(2,1)S(1)}, u32[]{:S(2)}, u32[]{:S(2)}) %all-to-all-start) | async-done | bytes 160 | tf_op jit(solution)/shard_map/all_to_all | solution.py:50
  40.8 21.5 %all-reduce = bf16[512]{0:T(512)(128)(2,1)S(1)} all-reduce(bf16[512]{0:T(512)(128)(2,1)S(1)} %dynamic-update-slice), channel_id=1, replica_groups=mesh['cluster'=16,'blk'=8] {'blk'}, use_global_device_ids=true, to_apply=%add | all-reduce | flops 512 | bytes 2048
  62.6 37.5 %all-gather.2.cloned.1.call-done = bf16[512,32,128]{2,1,0:T(8,128)(2,1)} async-done(((bf16[64,32,128]{2,1,0:T(8,128)(2,1)}), bf16[512,32,128]{2,1,0:T(8,128)(2,1)}) %all-gather.2.cloned.1.call-update) | async-done | bytes 4194320 | tf_op jit(solution)/shard_map/all_gather | solution.py:54
  100.0 70.3 %while.11 = (s32[]{:T(128)}, f32[8,8,512]{2,1,0:T(8,128)S(1)}, bf16[8,256,128]{2,1,0:T(8,128)(2,1)}, bf16[16384,128]{1,0:T(8,128)(2,1)}) while((s32[]{:T(128)}, f32[8,8,512]{2,1,0:T(8,128)S(1)}, bf16[8,256,128]{2,1,0:T(8,128)(2,1)}, bf16[16384,128]{1,0:T(8,128)(2,1)}) %tuple.27), condition=%wide.region_7.8_spmd.clone, body=%wide.region_4.7_spmd.sunk.clone | while | flops 1077936128 | bytes 5488705 | solution.py:25
  100.0 0.9 constant_dynamic-slice_fusion.3
  100.9 7.8 %fusion.19 = f32[8,32,512]{2,1,0:T(8,128)S(1)} fusion(bf16[8,32,128,1]{2,1,3,0:T(8,128)(2,1)S(1)} %bitcast.42, bf16[512,32,128]{2,1,0:T(8,128)(2,1)} %bitcast.46), kind=kOutput, calls=%fused_computation.6.clone.1.clone | convolution fusion | flops 1077805056 | bytes 4784128 | tf_op jit(solution)/shard_map/while/body/eval_jaxpr/dot_general | solution.py:18
  108.8 0.8 constant_dynamic-slice_fusion.3
  109.7 7.8 %fusion.19 = f32[8,32,512]{2,1,0:T(8,128)S(1)} fusion(bf16[8,32,128,1]{2,1,3,0:T(8,128)(2,1)S(1)} %bitcast.42, bf16[512,32,128]{2,1,0:T(8,128)(2,1)} %bitcast.46), kind=kOutput, calls=%fused_computation.6.clone.1.clone | convolution fusion | flops 1077805056 | bytes 4784128 | tf_op jit(solution)/shard_map/while/body/eval_jaxpr/dot_general | solution.py:18
  117.6 0.8 constant_dynamic-slice_fusion.3
  118.5 7.8 %fusion.19 = f32[8,32,512]{2,1,0:T(8,128)S(1)} fusion(bf16[8,32,128,1]{2,1,3,0:T(8,128)(2,1)S(1)} %bitcast.42, bf16[512,32,128]{2,1,0:T(8,128)(2,1)} %bitcast.46), kind=kOutput, calls=%fused_computation.6.clone.1.clone | convolution fusion | flops 1077805056 | bytes 4784128 | tf_op jit(solution)/shard_map/while/body/eval_jaxpr/dot_general | solution.py:18
  126.4 0.8 constant_dynamic-slice_fusion.3
  127.2 7.8 %fusion.19 = f32[8,32,512]{2,1,0:T(8,128)S(1)} fusion(bf16[8,32,128,1]{2,1,3,0:T(8,128)(2,1)S(1)} %bitcast.42, bf16[512,32,128]{2,1,0:T(8,128)(2,1)} %bitcast.46), kind=kOutput, calls=%fused_computation.6.clone.1.clone | convolution fusion | flops 1077805056 | bytes 4784128 | tf_op jit(solution)/shard_map/while/body/eval_jaxpr/dot_general | solution.py:18
  135.2 0.8 constant_dynamic-slice_fusion.3
  136.0 7.8 %fusion.19 = f32[8,32,512]{2,1,0:T(8,128)S(1)} fusion(bf16[8,32,128,1]{2,1,3,0:T(8,128)(2,1)S(1)} %bitcast.42, bf16[512,32,128]{2,1,0:T(8,128)(2,1)} %bitcast.46), kind=kOutput, calls=%fused_computation.6.clone.1.clone | convolution fusion | flops 1077805056 | bytes 4784128 | tf_op jit(solution)/shard_map/while/body/eval_jaxpr/dot_general | solution.py:18
  144.0 0.8 constant_dynamic-slice_fusion.3
  144.8 7.8 %fusion.19 = f32[8,32,512]{2,1,0:T(8,128)S(1)} fusion(bf16[8,32,128,1]{2,1,3,0:T(8,128)(2,1)S(1)} %bitcast.42, bf16[512,32,128]{2,1,0:T(8,128)(2,1)} %bitcast.46), kind=kOutput, calls=%fused_computation.6.clone.1.clone | convolution fusion | flops 1077805056 | bytes 4784128 | tf_op jit(solution)/shard_map/while/body/eval_jaxpr/dot_general | solution.py:18
  153.6 7.8 %fusion.19 = f32[8,32,512]{2,1,0:T(8,128)S(1)} fusion(bf16[8,32,128,1]{2,1,3,0:T(8,128)(2,1)S(1)} %bitcast.42, bf16[512,32,128]{2,1,0:T(8,128)(2,1)} %bitcast.46), kind=kOutput, calls=%fused_computation.6.clone.1.clone | convolution fusion | flops 1077805056 | bytes 4784128 | tf_op jit(solution)/shard_map/while/body/eval_jaxpr/dot_general | solution.py:18
  162.4 7.8 %fusion.19 = f32[8,32,512]{2,1,0:T(8,128)S(1)} fusion(bf16[8,32,128,1]{2,1,3,0:T(8,128)(2,1)S(1)} %bitcast.42, bf16[512,32,128]{2,1,0:T(8,128)(2,1)} %bitcast.46), kind=kOutput, calls=%fused_computation.6.clone.1.clone | convolution fusion | flops 1077805056 | bytes 4784128 | tf_op jit(solution)/shard_map/while/body/eval_jaxpr/dot_general | solution.py:18
  171.1 5.4 %all-to-all-start.2 = ((f32[16,4,1]{1,2,0:T(1,128)}), f32[16,4,1]{1,2,0:T(1,128)S(1)}, u32[]{:S(2)}, u32[]{:S(2)}) async-start(f32[16,4,1]{1,2,0:T(1,128)} %bitcast.12), calls=%async_computation.2 | async-start | bytes 16384 | tf_op jit(solution)/shard_map/all_to_all | solution.py:64
  176.5 5.5 %all-to-all-done.2 = f32[16,4,1]{1,2,0:T(1,128)S(1)} async-done(((f32[16,4,1]{1,2,0:T(1,128)}), f32[16,4,1]{1,2,0:T(1,128)S(1)}, u32[]{:S(2)}, u32[]{:S(2)}) %all-to-all-start.2) | async-done | bytes 288 | tf_op jit(solution)/shard_map/all_to_all | solution.py:64
  (50 shorter events, 10.8 us)
Async XLA Ops:
  6.5 93.5 %all-gather.2.cloned.1.call-start = ((), (), s32[]{:S(2)}) async-start(), calls=%async_computation.3 | async-start | bytes 4718592 | tf_op jit(solution)/shard_map/all_gather | solution.py:54
  30.5 9.9 %all-to-all-start = ((bf16[16,4,1]{1,2,0:T(2,128)(2,1)}), bf16[16,4,1]{1,2,0:T(2,128)(2,1)S(1)}, u32[]{:S(2)}, u32[]{:S(2)}) async-start(bf16[16,4,1]{1,2,0:T(2,128)(2,1)} %all_to_all.23), calls=%async_computation | async-start | bytes 16384 | tf_op jit(solution)/shard_map/all_to_all | solution.py:50
  100.0 84.0 %copy-start = (s32[32]{0:T(128)S(1)}, s32[32]{0:T(128)}, u32[]{:S(2)}) copy-start(s32[32]{0:T(128)} %param.7) | copy-start | bytes 388
  171.1 10.9 %all-to-all-start.2 = ((f32[16,4,1]{1,2,0:T(1,128)}), f32[16,4,1]{1,2,0:T(1,128)S(1)}, u32[]{:S(2)}, u32[]{:S(2)}) async-start(f32[16,4,1]{1,2,0:T(1,128)} %bitcast.12), calls=%async_computation.2 | async-start | bytes 16384 | tf_op jit(solution)/shard_map/all_to_all | solution.py:64
Sparse Core Ops, SparseCore 0:
  28.5 71.4 all-gather.1
where the time goes:
time: 192 us; the launch traced here: 191 us
  matrix products  62.6 us (33%)
  waiting for transfers between devices  46.5 us (24%)
  blocking collectives  38.1 us (20%)
  local copies, waits for them, and re-layouts  14.3 us (7%)
  between operations  14.1 us (7%)
  starting transfers between devices  9.73 us (5%)
  other arithmetic  5.72 us (3%)
    dot_general x8, matrix products, one_group(): lax.dot_general(queries, flat_visitors, (((1,), (1,)), ((), ())), preferr...  62.6 us
    all_gather x1, waiting for transfers between devices, body(): visitors = lax.all_gather(members, 'blk', axis=0, tiled=True)  37.5 us
    unnamed x1, blocking collectives  21.5 us
    all_to_all x1, blocking collectives, body(): lax.all_to_all(outgoing, 'cluster', split_axis=0, concat_axis=0, tiled=True)  16.6 us
    dynamic_slice x8, local copies, waits for them, and re-layouts, pair_scores(): result = lax.map(one_group, grouped)  6.8 us
    all_to_all x1, waiting for transfers between devices, body(): lax.all_to_all(score, 'cluster', split_axis=0, concat_axis=0, tiled=True)  5.47 us
    all_to_all x1, starting transfers between devices, body(): lax.all_to_all(score, 'cluster', split_axis=0, concat_axis=0, tiled=True)  5.39 us
    all_to_all x1, starting transfers between devices, body(): lax.all_to_all(outgoing_flags, 'cluster', split_axis=0, concat_axis=0, ti...  4.34 us
  transfers between devices with their start and end apart: 3, of which 3 were waited for; matrix products, arithmetic and copies ran while one was open for 2% of the time, Pallas kernels for 0%

commit v1 on v0

--- a/solution.py
+++ b/solution.py
@@ -51,7 +51,9 @@
     )
     flags = member_flags.astype(jnp.float32)
     own_ids = lax.axis_index("blk") * slot_count + jnp.arange(slot_count, dtype=jnp.int32)
-    visitors = lax.all_gather(members, "blk", axis=0, tiled=True)
+    visitors = jnp.concatenate(
+        lax.all_to_all(jnp.stack([members] * lax.axis_size("blk")), "blk", 0, 0), axis=0
+    )
     visitor_flags = lax.all_gather(member_flags, "blk", axis=0, tiled=True)
     other_ids = jnp.arange(visitors.shape[0], dtype=jnp.int32)
     weights = (own_ids[:, None] != other_ids[None, :]).astype(jnp.float32) * visitor_flags.astype(

time: 192 us -> 179 us (0.932)
  waiting for transfers between devices: 46.5 us -> 8.1 us
  blocking collectives: 38.1 us -> 69.9 us
  between operations: 14.1 us -> 0.68 us
  starting transfers between devices: 9.73 us -> 22.3 us
  local copies, waits for them, and re-layouts: 14.3 us -> 9.5 us
    all_gather x1 -> x0, waiting for transfers between devices: 37.5 us -> none  [body(): visitors = lax.all_gather(members, 'blk', axis=0, tiled=True)]
    unnamed x1, blocking collectives: 21.5 us -> 57.1 us
    all_to_all x0 -> x1, starting transfers between devices: none -> 7.33 us  [body(): lax.all_to_all(jnp.stack([members] * lax.axis_size('blk')), 'blk', 0, 0)]
    dynamic_slice x8, local copies, waits for them, and re-layouts: 6.8 us -> 0.09 us  [pair_scores(): result = lax.map(one_group, grouped)]
    all_to_all x1, blocking collectives: 16.6 us -> 12.8 us  [body(): lax.all_to_all(outgoing, 'cluster', split_axis=0, concat_axis=0, tiled=True)]
    another operation x0 -> x1, local copies, waits for them, and re-layouts: none -> 2.69 us  [body(): jnp.stack([members] * lax.axis_size('blk'))]
    all_to_all x1, starting transfers between devices: 5.39 us -> 8.07 us  [body(): lax.all_to_all(score, 'cluster', split_axis=0, concat_axis=0, tiled=True)]
    all_to_all x1, starting transfers between devices: 4.34 us -> 6.91 us  [body(): lax.all_to_all(outgoing_flags, 'cluster', split_axis=0, concat_axis=0, ti...]
  transfers between devices with their start and end apart: 3 -> 3, of which waited for: 3 -> 2; matrix products, arithmetic and copies ran while one was open for 2% -> 2% of each run, Pallas kernels for 0% -> 0%
where the time goes in v1:
time: 179 us; the launch traced here: 178 us
  blocking collectives  69.9 us (39%)
  matrix products  61.7 us (34%)
  starting transfers between devices  22.3 us (12%)
  local copies, waits for them, and re-layouts  9.5 us (5%)
  waiting for transfers between devices  8.1 us (5%)
  other arithmetic  5.72 us (3%)
    dot_general x8, matrix products, one_group(): lax.dot_general(queries, flat_visitors, (((1,), (1,)), ((), ())), preferr...  61.7 us
    unnamed x1, blocking collectives  57.1 us
    all_to_all x1, blocking collectives, body(): lax.all_to_all(outgoing, 'cluster', split_axis=0, concat_axis=0, tiled=True)  12.8 us
    all_to_all x1, starting transfers between devices, body(): lax.all_to_all(score, 'cluster', split_axis=0, concat_axis=0, tiled=True)  8.07 us
    all_to_all x1, starting transfers between devices, body(): lax.all_to_all(jnp.stack([members] * lax.axis_size('blk')), 'blk', 0, 0)  7.33 us
    all_to_all x1, starting transfers between devices, body(): lax.all_to_all(outgoing_flags, 'cluster', split_axis=0, concat_axis=0, ti...  6.91 us
    all_to_all x1, waiting for transfers between devices, body(): lax.all_to_all(score, 'cluster', split_axis=0, concat_axis=0, tiled=True)  5.53 us
  transfers between devices with their start and end apart: 3, of which 2 were waited for; matrix products, arithmetic and copies ran while one was open for 2% of the time, Pallas kernels for 0%

profile of v1, /device:TPU:1, one launch (start us, length us, event | category | flops | bytes accessed | tf_op | source)
XLA Modules:
  0.0 178.3 jit_solution(6578151583845348035)
XLA Ops:
  0.0 0.7 fusion.6
  0.8 0.8 select_reduce_fusion.1
  2.9 0.8 scatter_custom_fusion
  3.7 0.7 all_to_all.27
  4.4 6.9 %all-to-all-start = ((bf16[16,4,1]{1,2,0:T(2,128)(2,1)}), bf16[16,4,1]{1,2,0:T(2,128)(2,1)S(1)}, u32[]{:S(2)}, u32[]{:S(2)}) async-start(bf16[16,4,1]{1,2,0:T(2,128)(2,1)} %all_to_all.27), calls=%async_computation | async-start | bytes 16384 | tf_op jit(solution)/shard_map/all_to_all | solution.py:50
  11.4 2.8 %scatter_fusion = bf16[64,32,128]{2,1,0:T(8,128)(2,1)S(1)} fusion(bf16[64,32,128]{2,1,0:T(8,128)(2,1)S(1)} %broadcast_in_dim.11, s32[32]{0:T(128)S(1)} %fusion.7, bf16[32,32,128]{2,1,0:T(8,128)(2,1)} %param.5), kind=kCustom, calls=%fused_computation.2 | custom fusion | bytes 786560 | tf_op jit(solution)/shard_map/scatter | solution.py:43
  14.2 2.6 %all-to-all-done = bf16[16,4,1]{1,2,0:T(2,128)(2,1)S(1)} async-done(((bf16[16,4,1]{1,2,0:T(2,128)(2,1)}), bf16[16,4,1]{1,2,0:T(2,128)(2,1)S(1)}, u32[]{:S(2)}, u32[]{:S(2)}) %all-to-all-start) | async-done | bytes 160 | tf_op jit(solution)/shard_map/all_to_all | solution.py:50
  16.8 12.8 %all_to_all.32 = bf16[64,32,128]{2,1,0:T(8,128)(2,1)S(1)} all-to-all(bf16[64,32,128]{2,1,0:T(8,128)(2,1)S(1)} %scatter_fusion), channel_id=1, replica_groups=mesh['cluster'=16,'blk'=8] {'cluster'}, dimensions={0} | all-to-all | bytes 1048576 | tf_op jit(solution)/shard_map/all_to_all | solution.py:49
  29.6 2.7 %stack.2 = bf16[8,64,32,128]{3,2,1,0:T(8,128)(2,1)} broadcast(bf16[64,32,128]{2,1,0:T(8,128)(2,1)S(1)} %all_to_all.32), dimensions={1,2,3} | broadcast | bytes 4718592 | tf_op jit(solution)/shard_map/stack | solution.py:55
  32.3 7.3 %all-to-all-start.2 = ((bf16[8,64,32,128]{3,2,1,0:T(8,128)(2,1)}), bf16[8,64,32,128]{3,2,1,0:T(8,128)(2,1)}, u32[]{:S(2)}, u32[]{:S(2)}) async-start(bf16[8,64,32,128]{3,2,1,0:T(8,128)(2,1)} %stack.2), calls=%async_computation.2 | async-start | bytes 8388608 | tf_op jit(solution)/shard_map/all_to_all | solution.py:55
  41.2 57.1 %all-reduce = bf16[512]{0:T(512)(128)(2,1)S(1)} all-reduce(bf16[512]{0:T(512)(128)(2,1)S(1)} %dynamic-update-slice), channel_id=1, replica_groups=mesh['cluster'=16,'blk'=8] {'blk'}, use_global_device_ids=true, to_apply=%add | all-reduce | flops 512 | bytes 2048
  98.6 62.7 %while.11 = (s32[]{:T(128)}, f32[8,8,512]{2,1,0:T(8,128)S(1)}, bf16[8,256,128]{2,1,0:T(8,128)(2,1)S(1)}, bf16[16384,128]{1,0:T(8,128)(2,1)}) while((s32[]{:T(128)}, f32[8,8,512]{2,1,0:T(8,128)S(1)}, bf16[8,256,128]{2,1,0:T(8,128)(2,1)S(1)}, bf16[16384,128]{1,0:T(8,128)(2,1)}) %tuple.24), condition=%wide.region_7.8_spmd.clone, body=%wide.region_4.7_spmd.sunk.clone | while | flops 1077936128 | bytes 5488705 | solution.py:25
  98.6 7.7 %fusion.19 = f32[8,32,512]{2,1,0:T(8,128)S(1)} fusion(bf16[8,32,128,1]{2,1,3,0:T(8,128)(2,1)S(1)} %bitcast.42, bf16[512,32,128]{2,1,0:T(8,128)(2,1)} %bitcast.40), kind=kOutput, calls=%fused_computation.6.clone.1.clone | convolution fusion | flops 1077805056 | bytes 4784128 | tf_op jit(solution)/shard_map/while/body/eval_jaxpr/dot_general | solution.py:18
  106.5 7.7 %fusion.19 = f32[8,32,512]{2,1,0:T(8,128)S(1)} fusion(bf16[8,32,128,1]{2,1,3,0:T(8,128)(2,1)S(1)} %bitcast.42, bf16[512,32,128]{2,1,0:T(8,128)(2,1)} %bitcast.40), kind=kOutput, calls=%fused_computation.6.clone.1.clone | convolution fusion | flops 1077805056 | bytes 4784128 | tf_op jit(solution)/shard_map/while/body/eval_jaxpr/dot_general | solution.py:18
  114.3 7.7 %fusion.19 = f32[8,32,512]{2,1,0:T(8,128)S(1)} fusion(bf16[8,32,128,1]{2,1,3,0:T(8,128)(2,1)S(1)} %bitcast.42, bf16[512,32,128]{2,1,0:T(8,128)(2,1)} %bitcast.40), kind=kOutput, calls=%fused_computation.6.clone.1.clone | convolution fusion | flops 1077805056 | bytes 4784128 | tf_op jit(solution)/shard_map/while/body/eval_jaxpr/dot_general | solution.py:18
  122.2 7.7 %fusion.19 = f32[8,32,512]{2,1,0:T(8,128)S(1)} fusion(bf16[8,32,128,1]{2,1,3,0:T(8,128)(2,1)S(1)} %bitcast.42, bf16[512,32,128]{2,1,0:T(8,128)(2,1)} %bitcast.40), kind=kOutput, calls=%fused_computation.6.clone.1.clone | convolution fusion | flops 1077805056 | bytes 4784128 | tf_op jit(solution)/shard_map/while/body/eval_jaxpr/dot_general | solution.py:18
  130.0 7.7 %fusion.19 = f32[8,32,512]{2,1,0:T(8,128)S(1)} fusion(bf16[8,32,128,1]{2,1,3,0:T(8,128)(2,1)S(1)} %bitcast.42, bf16[512,32,128]{2,1,0:T(8,128)(2,1)} %bitcast.40), kind=kOutput, calls=%fused_computation.6.clone.1.clone | convolution fusion | flops 1077805056 | bytes 4784128 | tf_op jit(solution)/shard_map/while/body/eval_jaxpr/dot_general | solution.py:18
  137.8 7.7 %fusion.19 = f32[8,32,512]{2,1,0:T(8,128)S(1)} fusion(bf16[8,32,128,1]{2,1,3,0:T(8,128)(2,1)S(1)} %bitcast.42, bf16[512,32,128]{2,1,0:T(8,128)(2,1)} %bitcast.40), kind=kOutput, calls=%fused_computation.6.clone.1.clone | convolution fusion | flops 1077805056 | bytes 4784128 | tf_op jit(solution)/shard_map/while/body/eval_jaxpr/dot_general | solution.py:18
  145.7 7.7 %fusion.19 = f32[8,32,512]{2,1,0:T(8,128)S(1)} fusion(bf16[8,32,128,1]{2,1,3,0:T(8,128)(2,1)S(1)} %bitcast.42, bf16[512,32,128]{2,1,0:T(8,128)(2,1)} %bitcast.40), kind=kOutput, calls=%fused_computation.6.clone.1.clone | convolution fusion | flops 1077805056 | bytes 4784128 | tf_op jit(solution)/shard_map/while/body/eval_jaxpr/dot_general | solution.py:18
  153.5 7.7 %fusion.19 = f32[8,32,512]{2,1,0:T(8,128)S(1)} fusion(bf16[8,32,128,1]{2,1,3,0:T(8,128)(2,1)S(1)} %bitcast.42, bf16[512,32,128]{2,1,0:T(8,128)(2,1)} %bitcast.40), kind=kOutput, calls=%fused_computation.6.clone.1.clone | convolution fusion | flops 1077805056 | bytes 4784128 | tf_op jit(solution)/shard_map/while/body/eval_jaxpr/dot_general | solution.py:18
  162.2 8.1 %all-to-all-start.3 = ((f32[16,4,1]{1,2,0:T(1,128)}), f32[16,4,1]{1,2,0:T(1,128)S(1)}, u32[]{:S(2)}, u32[]{:S(2)}) async-start(f32[16,4,1]{1,2,0:T(1,128)} %bitcast.12), calls=%async_computation.3 | async-start | bytes 16384 | tf_op jit(solution)/shard_map/all_to_all | solution.py:66
  170.3 5.5 %all-to-all-done.3 = f32[16,4,1]{1,2,0:T(1,128)S(1)} async-done(((f32[16,4,1]{1,2,0:T(1,128)}), f32[16,4,1]{1,2,0:T(1,128)S(1)}, u32[]{:S(2)}, u32[]{:S(2)}) %all-to-all-start.3) | async-done | bytes 288 | tf_op jit(solution)/shard_map/all_to_all | solution.py:66
  176.3 0.7 reduce.5
  177.1 0.7 gather_fusion
  (52 shorter events, 5.3 us)
Async XLA Ops:
  4.4 12.4 %all-to-all-start = ((bf16[16,4,1]{1,2,0:T(2,128)(2,1)}), bf16[16,4,1]{1,2,0:T(2,128)(2,1)S(1)}, u32[]{:S(2)}, u32[]{:S(2)}) async-start(bf16[16,4,1]{1,2,0:T(2,128)(2,1)} %all_to_all.27), calls=%async_computation | async-start | bytes 16384 | tf_op jit(solution)/shard_map/all_to_all | solution.py:50
  32.3 7.3 %copy-start.1 = (u32[128]{0:T(128)S(1)}, u32[128]{0:T(128)}, u32[]{:S(2)}) copy-start(u32[128]{0:T(128)} %constant.49) | copy-start | bytes 1540
  32.3 66.3 %all-to-all-start.2 = ((bf16[8,64,32,128]{3,2,1,0:T(8,128)(2,1)}), bf16[8,64,32,128]{3,2,1,0:T(8,128)(2,1)}, u32[]{:S(2)}, u32[]{:S(2)}) async-start(bf16[8,64,32,128]{3,2,1,0:T(8,128)(2,1)} %stack.2), calls=%async_computation.2 | async-start | bytes 8388608 | tf_op jit(solution)/shard_map/all_to_all | solution.py:55
  98.6 79.2 %copy-start = (s32[32]{0:T(128)S(1)}, s32[32]{0:T(128)}, u32[]{:S(2)}) copy-start(s32[32]{0:T(128)} %param.7) | copy-start | bytes 388
  162.2 13.6 %all-to-all-start.3 = ((f32[16,4,1]{1,2,0:T(1,128)}), f32[16,4,1]{1,2,0:T(1,128)S(1)}, u32[]{:S(2)}, u32[]{:S(2)}) async-start(f32[16,4,1]{1,2,0:T(1,128)} %bitcast.12), calls=%async_computation.3 | async-start | bytes 16384 | tf_op jit(solution)/shard_map/all_to_all | solution.py:66
